TPU v7x, 32 devices: a whole 2x2x4 slice. The times are simulated.
32 devices in a mesh: tm: 8 (over z, x), col: 4 (over y, core).
Axes of the slice: x: 2, y: 2, z: 4, core: 2. Of those that a mesh axis runs over, the one named last changes fastest.
Arguments:
- jacobians: float32 [96, 512, 512], P('tm'), may hold values from -0.05 to 1.05
- increments: float32 [96, 512], P('tm'), may hold values from -1.5 to 1.5
- initial: float32 [512], P('col'), may hold values from -6 to 6
Outputs:
- states: float32 [96, 512], P('tm', 'col')
All inputs are finite; a program needn't handle non-finite values.
Results may differ from a plain program's by a relative error of at most 0.0003.
Values sent between devices are 32-bit elements; how exact they have to be, the bound alone decides.
No kernel may reach another device: no remote copies, remote signals or barrier semaphores. Data moves between devices by JAX's collectives and lax.ppermute only.
A program may use at most 128 MiB of HBM per device.

v0:
```python
import jax
import jax.numpy as jnp
from jax import lax
from jax.sharding import PartitionSpec as P


def from_behind(block, axis, distance):
    devices = range(lax.axis_size(axis))
    route = [(i - distance, i) for i in devices if i - distance in devices]
    return lax.ppermute(block, axis, route)


def matmul(left, right):
    return jnp.dot(left, right, precision=lax.Precision.HIGHEST, preferred_element_type=jnp.float32)


def body(jacobians, increments, initial):
    part_cols = initial.shape[0]
    column_index = lax.axis_index("col")
    segment_index = lax.axis_index("tm")
    rounds = (lax.axis_size("tm") - 1).bit_length()
    first_col = column_index * part_cols

    def own_cols(matrix):
        return lax.dynamic_slice_in_dim(matrix, first_col, part_cols, matrix.ndim - 1)

    def advance_map(running, inputs):
        step_jac, step_inc = inputs
        return ((matmul(step_jac, running[0]), matmul(step_jac, running[1]) + step_inc), None)

    composed, _ = lax.scan(
        advance_map, (own_cols(jacobians[0]), increments[0]), (jacobians[1:], increments[1:])
    )
    acc_map, acc_off = composed
    for level_index in range(rounds):
        distance = 1 << level_index
        recv_map, recv_off = from_behind((acc_map, acc_off), "tm", distance)

        def fold_columns(running, col_block, first_row, recv_map=recv_map, recv_off=recv_off):
            return (matmul(col_block, recv_map), running[1] + matmul(col_block, recv_off))

        new_map, new_off = fold_columns(
            (jnp.zeros_like(acc_map), acc_off),
            lax.all_gather(acc_map, "col", axis=1, tiled=True),
            jnp.int32(0),
        )
        active = segment_index >= distance
        acc_map = jnp.where(active, new_map, acc_map)
        acc_off = jnp.where(active, new_off, acc_off)
    end_part = matmul(acc_map, initial)
    end_mine = lax.psum_scatter(end_part, "col", scatter_dimension=0, tiled=True) + own_cols(
        acc_off
    )
    handed = from_behind(end_mine, "tm", 1)
    start_mine = jnp.where(segment_index == 0, initial, handed)
    start_full = lax.all_gather(start_mine, "col", axis=0, tiled=True)

    def advance_state(current, inputs):
        step_jac, step_inc = inputs
        following = matmul(step_jac, current) + step_inc
        return (following, own_cols(following))

    _, leading = lax.scan(advance_state, start_full, (jacobians[:-1], increments[:-1]))
    return jnp.concatenate([leading, end_mine[None, :]], axis=0)


def solution(mesh):
    return jax.shard_map(
        body,
        mesh=mesh,
        in_specs=(P("tm", None, None), P("tm", None), P("col")),
        out_specs=P("tm", "col"),
        check_vma=False,
    )
```

profile of v0, /device:TPU:25, one launch (start us, length us, event | category | flops | bytes accessed | tf_op | source)
XLA Modules:
  0.0 202.7 jit_solution(5260583161376502509)
XLA Ops:
  6.5 17.6 %fusion.15 = (f32[11,512,512]{2,1,0:T(8,128)}, f32[11,512,512]{2,1,0:T(8,128)}) fusion(f32[12,512,512]{2,1,0:T(8,128)} %param.7), kind=kLoop, calls=%fused_computation.28 | loop fusion | bytes 46137344 | tf_op jit(solution)/shard_map/slice | solution.py:63
  24.2 49.5 %while.26 = (s32[]{:T(128)}, f32[512,128]{1,0:T(8,128)S(1)}, f32[512]{0:T(512)S(1)}, f32[11,512,512]{2,1,0:T(8,128)}, f32[11,512]{1,0:T(8,128)S(1)}, /*index=5*/s32[]{:T(128)}) while((s32[]{:T(128)}, f32[512,128]{1,0:T(8,128)S(1)}, f32[512]{0:T(512)S(1)}, f32[11,512,512]{2,1,0:T(8,128)}, f32[11,512]{1,0:T(8,128)S(1)}, ...), condition=%wide.region_1.2_spmd, body=%wide.region_0.1_spmd.sunk | while | flops 405799424 | bytes 3161161 | solution.py:31
  26.5 2.2 %fusion.49 = f32[512,128]{1,0:T(8,128)S(1)} fusion(f32[512,128]{1,0:T(8,128)S(1)} %copy.24, f32[11,512,512]{2,1,0:T(8,128)} %get-tuple-element.219, s32[]{:T(128)} %get-tuple-element.210), kind=kOutput, calls=%fused_computation.2.clone.1 | convolution fusion | flops 402653184 | bytes 1573376 | tf_op jit(solution)/shard_map/while/body/eval_jaxpr/dot_general | solution.py:14
  35.5 2.2 %fusion.49 = f32[512,128]{1,0:T(8,128)S(1)} fusion(f32[512,128]{1,0:T(8,128)S(1)} %copy.24, f32[11,512,512]{2,1,0:T(8,128)} %get-tuple-element.219, s32[]{:T(128)} %get-tuple-element.210), kind=kOutput, calls=%fused_computation.2.clone.1 | convolution fusion | flops 402653184 | bytes 1573376 | tf_op jit(solution)/shard_map/while/body/eval_jaxpr/dot_general | solution.py:14
  40.0 2.2 %fusion.49 = f32[512,128]{1,0:T(8,128)S(1)} fusion(f32[512,128]{1,0:T(8,128)S(1)} %copy.24, f32[11,512,512]{2,1,0:T(8,128)} %get-tuple-element.219, s32[]{:T(128)} %get-tuple-element.210), kind=kOutput, calls=%fused_computation.2.clone.1 | convolution fusion | flops 402653184 | bytes 1573376 | tf_op jit(solution)/shard_map/while/body/eval_jaxpr/dot_general | solution.py:14
  49.0 2.2 %fusion.49 = f32[512,128]{1,0:T(8,128)S(1)} fusion(f32[512,128]{1,0:T(8,128)S(1)} %copy.24, f32[11,512,512]{2,1,0:T(8,128)} %get-tuple-element.219, s32[]{:T(128)} %get-tuple-element.210), kind=kOutput, calls=%fused_computation.2.clone.1 | convolution fusion | flops 402653184 | bytes 1573376 | tf_op jit(solution)/shard_map/while/body/eval_jaxpr/dot_general | solution.py:14
  62.5 2.2 %fusion.49 = f32[512,128]{1,0:T(8,128)S(1)} fusion(f32[512,128]{1,0:T(8,128)S(1)} %copy.24, f32[11,512,512]{2,1,0:T(8,128)} %get-tuple-element.219, s32[]{:T(128)} %get-tuple-element.210), kind=kOutput, calls=%fused_computation.2.clone.1 | convolution fusion | flops 402653184 | bytes 1573376 | tf_op jit(solution)/shard_map/while/body/eval_jaxpr/dot_general | solution.py:14
  74.5 3.1 %collective-permute-start = (f32[512,128]{1,0:T(8,128)}, f32[512,128]{1,0:T(8,128)S(1)}, u32[]{:S(2)}, u32[]{:S(2)}) collective-permute-start(f32[512,128]{1,0:T(8,128)} %copy-done), channel_id=1, source_target_pairs={{0,4},{4,8},{8,12},{12,16},{16,20},{20,24},{24,28},{1,5},{5,9},{9,... | collective-permute-start | bytes 786440 | tf_op jit(solution)/shard_map/ppermute | solution.py:10
  77.7 7.1 %collective-permute-done = f32[512,128]{1,0:T(8,128)S(1)} collective-permute-done((f32[512,128]{1,0:T(8,128)}, f32[512,128]{1,0:T(8,128)S(1)}, u32[]{:S(2)}, u32[]{:S(2)}) %collective-permute-start) | collective-permute-done | bytes 262176 | tf_op jit(solution)/shard_map/ppermute | solution.py:10
  84.7 8.1 %all-gather.5.cloned.1.call-done = f32[512,512]{1,0:T(8,128)} async-done(((f32[512,128]{1,0:T(8,128)}), f32[512,512]{1,0:T(8,128)}) %all-gather.5.cloned.1.call-update) | async-done | bytes 1048592 | tf_op jit(solution)/shard_map/all_gather | solution.py:44
  92.8 2.9 %convolution_select_fusion.2 = f32[512,128]{1,0:T(8,128)} fusion(f32[512,128]{1,0:T(8,128)} %copy-done, f32[512,512]{1,0:T(8,128)} %all-gather.5.cloned.1.call-done, f32[512,128]{1,0:T(8,128)S(1)} %collective-permute-done, pred[]{:T(512)S(6)} %ge.11), kind=kOutput, calls=%fused_computation.17 | convolution fusion | flops 402718720 | bytes 1835009 | tf_op jit(solution)/shard_map/dot_general | solution.py:14
  97.1 8.4 %collective-permute-done.1 = f32[512,128]{1,0:T(8,128)S(1)} collective-permute-done((f32[512,128]{1,0:T(8,128)}, f32[512,128]{1,0:T(8,128)S(1)}, u32[]{:S(2)}, u32[]{:S(2)}) %collective-permute-start.1) | collective-permute-done | bytes 262176 | tf_op jit(solution)/shard_map/ppermute | solution.py:10
  105.5 7.2 %all-gather.7.cloned.1.call-done = f32[512,512]{1,0:T(8,128)} async-done(((f32[512,128]{1,0:T(8,128)}), f32[512,512]{1,0:T(8,128)}) %all-gather.7.cloned.1.call-update) | async-done | bytes 1048592 | tf_op jit(solution)/shard_map/all_gather | solution.py:44
  112.7 2.9 %convolution_select_fusion.1 = f32[512,128]{1,0:T(8,128)} fusion(f32[512,128]{1,0:T(8,128)} %convolution_select_fusion.2, f32[512,512]{1,0:T(8,128)} %all-gather.7.cloned.1.call-done, f32[512,128]{1,0:T(8,128)S(1)} %collective-permute-done.1, pred[]{:T(512)S(6)} %ge.10), kind=kOutput, calls=%fused_computation.16 | convolution fusion | flops 402718720 | bytes 1835009 | tf_op jit(solution)/shard_map/dot_general | solution.py:14
  115.7 3.1 %collective-permute-start.3 = (f32[512]{0:T(512)S(1)}, f32[512]{0:T(512)S(1)}, u32[]{:S(2)}, u32[]{:S(2)}) collective-permute-start(f32[512]{0:T(512)S(1)} %get-tuple-element.108), channel_id=1, source_target_pairs={{0,4},{4,8},{8,12},{12,16},{16,20},{20,24},{24,28},{1,5},{5,9},{9,... | collective-permute-start | bytes 6152 | tf_op jit(solution)/shard_map/ppermute | solution.py:10
  120.9 2.2 %fusion.17 = f32[1,512]{1,0:T(1,128)S(1)} fusion(f32[512,512]{1,0:T(8,128)} %all-gather.5.cloned.1.call-done, f32[512,1]{0,1:T(1,128)S(1)} %bitcast.89), kind=kOutput, calls=%fused_computation.30 | convolution fusion | flops 3145728 | bytes 1052672 | tf_op jit(solution)/shard_map/dot_general | solution.py:14
  124.5 3.4 %collective-permute-done.4 = f32[512]{0:T(512)S(1)} collective-permute-done((f32[512]{0:T(512)S(1)}, f32[512]{0:T(512)S(1)}, u32[]{:S(2)}, u32[]{:S(2)}) %collective-permute-start.4) | collective-permute-done | bytes 2080 | tf_op jit(solution)/shard_map/ppermute | solution.py:10
  127.9 2.3 %fusion.18 = f32[1,512]{1,0:T(1,128)S(1)} fusion(f32[512,512]{1,0:T(8,128)} %all-gather.7.cloned.1.call-done, f32[512,1]{0,1:T(1,128)S(1)} %bitcast.90), kind=kOutput, calls=%fused_computation.31 | convolution fusion | flops 3145728 | bytes 1052672 | tf_op jit(solution)/shard_map/dot_general | solution.py:14
  137.6 11.9 %collective-permute-done.2 = f32[512,128]{1,0:T(8,128)S(1)} collective-permute-done((f32[512,128]{1,0:T(8,128)}, f32[512,128]{1,0:T(8,128)S(1)}, u32[]{:S(2)}, u32[]{:S(2)}) %collective-permute-start.2) | collective-permute-done | bytes 262176 | tf_op jit(solution)/shard_map/ppermute | solution.py:10
  149.5 2.2 %convolution_select_fusion = f32[512,128]{1,0:T(8,128)S(1)} fusion(f32[512,128]{1,0:T(8,128)} %convolution_select_fusion.1, f32[512,512]{1,0:T(8,128)} %all-gather.9.cloned.1.call-done, f32[512,128]{1,0:T(8,128)S(1)} %collective-permute-done.2, pred[]{:T(512)S(6)} %ge.9), kind=kOutput, calls=%fused_computation.15 | convolution fusion | flops 402718720 | bytes 1835009 | tf_op jit(solution)/shard_map/dot_general | solution.py:14
  152.1 5.5 %all-reduce = f32[512]{0:T(512)S(1)} all-reduce(f32[512]{0:T(512)S(1)} %bitcast.87), channel_id=2, replica_groups=mesh['tm'=8,'col'=4] {'col'}, use_global_device_ids=true, to_apply=%region_2.3.clone | all-reduce | flops 512 | bytes 4096
  159.8 3.1 %collective-permute-done.6 = f32[128]{0:T(128)S(1)} collective-permute-done((f32[128]{0:T(128)S(1)}, f32[128]{0:T(128)S(1)}, u32[]{:S(2)}, u32[]{:S(2)}) %collective-permute-start.6) | collective-permute-done | bytes 544 | tf_op jit(solution)/shard_map/ppermute | solution.py:10
  162.9 6.9 %all-gather = f32[4,1,128]{2,1,0:T(1,128)S(1)} all-gather(f32[1,1,128]{2,1,0:T(1,128)S(1)} %fusion.12), channel_id=1, replica_groups=mesh['tm'=8,'col'=4] {'col'}, dimensions={0}, use_global_device_ids=true | all-gather | bytes 2560 | tf_op jit(solution)/shard_map/all_gather | solution.py:56
  169.8 25.8 %while.27 = (s32[]{:T(128)}, f32[512]{0:T(512)S(1)}, f32[11,128]{1,0:T(8,128)S(1)}, f32[11,512,512]{2,1,0:T(8,128)}, f32[11,512]{1,0:T(8,128)S(1)}, /*index=5*/s32[]{:T(128)}, s32[]{:T(128)}, s32[]{:T(128)}) while((s32[]{:T(128)}, f32[512]{0:T(512)S(1)}, f32[11,128]{1,0:T(8,128)S(1)}, f32[11,512,512]{2,1,0:T(8,128)}, f32[11,512]{1,0:T(8,128)S(1)}, ...), condition=%wide.region_4.5_spmd, body=%wide.region_3.4_spmd.sunk | while | flops 3146242 | bytes 1065569 | solution.py:63
  (143 shorter events, 79.1 us)
Async XLA Ops:
  6.5 86.3 %all-gather.5.cloned.1.call-start = ((), (), s32[]{:S(2)}) async-start(), calls=%async_computation | async-start | bytes 1310720 | tf_op jit(solution)/shard_map/all_gather | solution.py:44
  6.5 17.6 %copy-start.1 = (f32[12,512]{1,0:T(8,128)S(1)}, f32[12,512]{1,0:T(8,128)}, u32[]{:S(2)}) copy-start(f32[12,512]{1,0:T(8,128)} %param.8) | copy-start | bytes 73732
  6.5 17.6 %slice-start = ((f32[12,512,512]{2,1,0:T(8,128)}), f32[1,512,512]{2,1,0:T(8,128)S(1)}, s32[]{:S(2)}) async-start(f32[12,512,512]{2,1,0:T(8,128)} %param.7), calls=%async_computation.3 | async-start | bytes 2097152 | tf_op jit(solution)/shard_map/slice | solution.py:32
  6.5 17.7 %slice-start.1 = ((f32[12,512]{1,0:T(8,128)}), f32[1,512]{1,0:T(1,128)S(1)}, s32[]{:S(2)}) async-start(f32[12,512]{1,0:T(8,128)} %param.8), calls=%async_computation.4 | async-start | bytes 4096 | tf_op jit(solution)/shard_map/slice | solution.py:32
  24.1 107.3 %copy-start.3 = (u32[32]{0:T(128)S(1)}, u32[32]{0:T(128)}, u32[]{:S(2)}) copy-start(u32[32]{0:T(128)} %constant.58) | copy-start | bytes 388
  24.2 127.5 %copy-start.2 = (f32[128]{0:T(128)S(1)}, f32[128]{0:T(128)}, u32[]{:S(2)}) copy-start(f32[128]{0:T(128)} %param.9) | copy-start | bytes 1540
  73.7 0.7 copy-start
  74.5 38.3 %all-gather.7.cloned.1.call-start = ((), (), s32[]{:S(2)}) async-start(), calls=%async_computation.1 | async-start | bytes 1310720 | tf_op jit(solution)/shard_map/all_gather | solution.py:44
  74.5 10.2 %collective-permute-start = (f32[512,128]{1,0:T(8,128)}, f32[512,128]{1,0:T(8,128)S(1)}, u32[]{:S(2)}, u32[]{:S(2)}) collective-permute-start(f32[512,128]{1,0:T(8,128)} %copy-done), channel_id=1, source_target_pairs={{0,4},{4,8},{8,12},{12,16},{16,20},{20,24},{24,28},{1,5},{5,9},{9,... | collective-permute-start | bytes 786440 | tf_op jit(solution)/shard_map/ppermute | solution.py:10
  95.8 39.6 %all-gather.9.cloned.1.call-start = ((), (), s32[]{:S(2)}) async-start(), calls=%async_computation.2 | async-start | bytes 1310720 | tf_op jit(solution)/shard_map/all_gather | solution.py:44
  95.8 9.7 %collective-permute-start.1 = (f32[512,128]{1,0:T(8,128)}, f32[512,128]{1,0:T(8,128)S(1)}, u32[]{:S(2)}, u32[]{:S(2)}) collective-permute-start(f32[512,128]{1,0:T(8,128)} %convolution_select_fusion.2), channel_id=1, source_target_pairs={{0,8},{4,12},{8,16},{12,20},{16,24},{20,28},{1,9},{5,13},{9,17},{1... | collective-permute-start | bytes 786440 | tf_op jit(solution)/shard_map/ppermute | solution.py:10
  115.7 5.2 %collective-permute-start.3 = (f32[512]{0:T(512)S(1)}, f32[512]{0:T(512)S(1)}, u32[]{:S(2)}, u32[]{:S(2)}) collective-permute-start(f32[512]{0:T(512)S(1)} %get-tuple-element.108), channel_id=1, source_target_pairs={{0,4},{4,8},{8,12},{12,16},{16,20},{20,24},{24,28},{1,5},{5,9},{9,... | collective-permute-start | bytes 6152 | tf_op jit(solution)/shard_map/ppermute | solution.py:10
  123.2 4.7 %collective-permute-start.4 = (f32[512]{0:T(512)S(1)}, f32[512]{0:T(512)S(1)}, u32[]{:S(2)}, u32[]{:S(2)}) collective-permute-start(f32[512]{0:T(512)S(1)} %add_select_fusion.2), channel_id=1, source_target_pairs={{0,8},{4,12},{8,16},{12,20},{16,24},{20,28},{1,9},{5,13},{9,17},{1... | collective-permute-start | bytes 6152 | tf_op jit(solution)/shard_map/ppermute | solution.py:10
  130.2 5.2 %collective-permute-start.5 = (f32[512]{0:T(512)S(1)}, f32[512]{0:T(512)S(1)}, u32[]{:S(2)}, u32[]{:S(2)}) collective-permute-start(f32[512]{0:T(512)S(1)} %add_select_fusion.1), channel_id=1, source_target_pairs={{0,16},{4,20},{8,24},{12,28},{1,17},{5,21},{9,25},{13,29},{2,18},{... | collective-permute-start | bytes 6152 | tf_op jit(solution)/shard_map/ppermute | solution.py:10
  132.7 16.8 %collective-permute-start.2 = (f32[512,128]{1,0:T(8,128)}, f32[512,128]{1,0:T(8,128)S(1)}, u32[]{:S(2)}, u32[]{:S(2)}) collective-permute-start(f32[512,128]{1,0:T(8,128)} %convolution_select_fusion.1), channel_id=1, source_target_pairs={{0,16},{4,20},{8,24},{12,28},{1,17},{5,21},{9,25},{13,29},{2,18},{... | collective-permute-start | bytes 786440 | tf_op jit(solution)/shard_map/ppermute | solution.py:10
  157.7 5.2 %collective-permute-start.6 = (f32[128]{0:T(128)S(1)}, f32[128]{0:T(128)S(1)}, u32[]{:S(2)}, u32[]{:S(2)}) collective-permute-start(f32[128]{0:T(128)S(1)} %dynamic-slice_add_fusion), channel_id=1, source_target_pairs={{0,4},{4,8},{8,12},{12,16},{16,20},{20,24},{24,28},{1,5},{5,9},{9,... | collective-permute-start | bytes 1544 | tf_op jit(solution)/shard_map/ppermute | solution.py:10
Sparse Core Ops, SparseCore 0:
  74.6 18.1 all-gather.4
  95.9 16.8 all-gather.6
  115.8 16.8 all-gather.8
where the time goes:
time: 205 us; the launch traced here: 203 us
  matrix products  87.8 us (43%)
  waiting for transfers between devices  52.8 us (26%)
  local copies, waits for them, and re-layouts  20.7 us (10%)
  between operations  14 us (7%)
  starting transfers between devices  13.6 us (7%)
  blocking collectives  12.4 us (6%)
    dot_general x40, matrix products, matmul(): jnp.dot(left, right, precision=lax.Precision.HIGHEST, preferred_element_t...  87.8 us
    ppermute x7, waiting for transfers between devices, from_behind(): return lax.ppermute(block, axis, route)  37.4 us
    slice x1, local copies, waits for them, and re-layouts, body(): jacobians[:-1]  17.6 us
    all_gather x3, waiting for transfers between devices, body(): lax.all_gather(acc_map, 'col', axis=1, tiled=True)  15.3 us
    ppermute x7, starting transfers between devices, from_behind(): return lax.ppermute(block, axis, route)  13.5 us
    all_gather x1, blocking collectives, body(): start_full = lax.all_gather(start_mine, 'col', axis=0, tiled=True)  6.9 us
    unnamed x1, blocking collectives  5.5 us
  transfers between devices with their start and end apart: 10, of which 9 were waited for; matrix products, arithmetic and copies ran while one was open for 4% of the time, Pallas kernels for 0%

commit v1 on v0

--- a/solution.py
+++ b/solution.py
@@ -2,6 +2,22 @@
 import jax.numpy as jnp
 from jax import lax
 from jax.sharding import PartitionSpec as P
+
+
+def reach_waves(values):
+    panels = [values]
+    count_all = lax.psum(1, "col")
+    for rr in range(1, count_all):
+        panels.append(
+            lax.ppermute(
+                panels[rr - 1],
+                axis_name="col",
+                perm=[(j, (j - 1) % count_all) for j in range(count_all)],
+            )
+        )
+    row_out = jnp.concatenate(panels, axis=1)
+    y1 = lax.axis_index("col")
+    return jnp.roll(row_out, shift=y1 * values.shape[1], axis=1)
 
 
 def from_behind(block, axis, distance):
@@ -40,9 +56,7 @@
             return (matmul(col_block, recv_map), running[1] + matmul(col_block, recv_off))
 
         new_map, new_off = fold_columns(
-            (jnp.zeros_like(acc_map), acc_off),
-            lax.all_gather(acc_map, "col", axis=1, tiled=True),
-            jnp.int32(0),
+            (jnp.zeros_like(acc_map), acc_off), reach_waves(acc_map), jnp.int32(0)
         )
         active = segment_index >= distance
         acc_map = jnp.where(active, new_map, acc_map)

time: 205 us -> 187 us (0.912)
  between operations: 14 us -> 0.93 us
  matrix products: 87.8 us -> 77.9 us
  starting transfers between devices: 13.6 us -> 18.7 us
  waiting for transfers between devices: 52.8 us -> 48.5 us
  other arithmetic: 0.83 us -> 4.42 us
    ppermute x0 -> x9, waiting for transfers between devices: none -> 34 us  [reach_waves(): lax.ppermute(panels[rr - 1], axis_name='col', perm=[(j, (j - 1) % count_a...]
    ppermute x7, waiting for transfers between devices: 37.4 us -> 14.6 us  [from_behind(): return lax.ppermute(block, axis, route)]
    all_gather x3 -> x0, waiting for transfers between devices: 15.3 us -> none  [body(): lax.all_gather(acc_map, 'col', axis=1, tiled=True)]
    dot_general x40, matrix products: 87.8 us -> 77.9 us  [matmul(): jnp.dot(left, right, precision=lax.Precision.HIGHEST, preferred_element_t...]
    ppermute x0 -> x9, starting transfers between devices: none -> 6.08 us  [reach_waves(): lax.ppermute(panels[rr - 1], axis_name='col', perm=[(j, (j - 1) % count_a...]
    concatenate x0 -> x3, other arithmetic: none -> 3.61 us  [reach_waves(): return jnp.roll(row_out, shift=y1 * values.shape[1], axis=1)]
  transfers between devices with their start and end apart: 10 -> 16, of which waited for: 9 -> 13; matrix products, arithmetic and copies ran while one was open for 4% -> 4% of each run, Pallas kernels for 0% -> 0%
where the time goes in v1:
time: 187 us; the launch traced here: 185 us
  matrix products  77.9 us (42%)
  waiting for transfers between devices  48.5 us (26%)
  local copies, waits for them, and re-layouts  20.1 us (11%)
  starting transfers between devices  18.7 us (10%)
  blocking collectives  14 us (7%)
  other arithmetic  4.42 us (2%)
    dot_general x40, matrix products, matmul(): jnp.dot(left, right, precision=lax.Precision.HIGHEST, preferred_element_t...  77.9 us
    ppermute x9, waiting for transfers between devices, reach_waves(): lax.ppermute(panels[rr - 1], axis_name='col', perm=[(j, (j - 1) % count_a...  34 us
    slice x1, local copies, waits for them, and re-layouts, body(): jacobians[:-1]  17.6 us
    ppermute x7, waiting for transfers between devices, from_behind(): return lax.ppermute(block, axis, route)  14.6 us
    ppermute x7, starting transfers between devices, from_behind(): return lax.ppermute(block, axis, route)  12.6 us
    unnamed x1, blocking collectives  7.03 us
    all_gather x1, blocking collectives, body(): start_full = lax.all_gather(start_mine, 'col', axis=0, tiled=True)  6.99 us
    ppermute x9, starting transfers between devices, reach_waves(): lax.ppermute(panels[rr - 1], axis_name='col', perm=[(j, (j - 1) % count_a...  6.08 us
  transfers between devices with their start and end apart: 16, of which 13 were waited for; matrix products, arithmetic and copies ran while one was open for 4% of the time, Pallas kernels for 0%

profile of v1, /device:TPU:25, one launch (start us, length us, event | category | flops | bytes accessed | tf_op | source)
XLA Modules:
  0.0 185.3 jit_solution(10386349933675849329)
XLA Ops:
  0.0 17.6 %fusion.36 = (f32[11,512,512]{2,1,0:T(8,128)}, f32[11,512,512]{2,1,0:T(8,128)}) fusion(f32[12,512,512]{2,1,0:T(8,128)} %param.9), kind=kLoop, calls=%fused_computation.73 | loop fusion | bytes 46137344 | tf_op jit(solution)/shard_map/slice | solution.py:77
  17.7 49.5 %while.26 = (s32[]{:T(128)}, f32[512,128]{1,0:T(8,128)S(1)}, f32[512]{0:T(512)S(1)}, f32[11,512,512]{2,1,0:T(8,128)}, f32[11,512]{1,0:T(8,128)S(1)}, /*index=5*/s32[]{:T(128)}) while((s32[]{:T(128)}, f32[512,128]{1,0:T(8,128)S(1)}, f32[512]{0:T(512)S(1)}, f32[11,512,512]{2,1,0:T(8,128)}, f32[11,512]{1,0:T(8,128)S(1)}, ...), condition=%wide.region_1.2_spmd, body=%wide.region_0.1_spmd.sunk | while | flops 405799424 | bytes 3161161 | solution.py:47
  19.9 2.2 %fusion.70 = f32[512,128]{1,0:T(8,128)S(1)} fusion(f32[512,128]{1,0:T(8,128)S(1)} %copy.26, f32[11,512,512]{2,1,0:T(8,128)} %get-tuple-element.220, s32[]{:T(128)} %get-tuple-element.211), kind=kOutput, calls=%fused_computation.2.clone.1 | convolution fusion | flops 402653184 | bytes 1573376 | tf_op jit(solution)/shard_map/while/body/eval_jaxpr/dot_general | solution.py:30
  29.0 2.2 %fusion.70 = f32[512,128]{1,0:T(8,128)S(1)} fusion(f32[512,128]{1,0:T(8,128)S(1)} %copy.26, f32[11,512,512]{2,1,0:T(8,128)} %get-tuple-element.220, s32[]{:T(128)} %get-tuple-element.211), kind=kOutput, calls=%fused_computation.2.clone.1 | convolution fusion | flops 402653184 | bytes 1573376 | tf_op jit(solution)/shard_map/while/body/eval_jaxpr/dot_general | solution.py:30
  38.0 2.2 %fusion.70 = f32[512,128]{1,0:T(8,128)S(1)} fusion(f32[512,128]{1,0:T(8,128)S(1)} %copy.26, f32[11,512,512]{2,1,0:T(8,128)} %get-tuple-element.220, s32[]{:T(128)} %get-tuple-element.211), kind=kOutput, calls=%fused_computation.2.clone.1 | convolution fusion | flops 402653184 | bytes 1573376 | tf_op jit(solution)/shard_map/while/body/eval_jaxpr/dot_general | solution.py:30
  47.0 2.2 %fusion.70 = f32[512,128]{1,0:T(8,128)S(1)} fusion(f32[512,128]{1,0:T(8,128)S(1)} %copy.26, f32[11,512,512]{2,1,0:T(8,128)} %get-tuple-element.220, s32[]{:T(128)} %get-tuple-element.211), kind=kOutput, calls=%fused_computation.2.clone.1 | convolution fusion | flops 402653184 | bytes 1573376 | tf_op jit(solution)/shard_map/while/body/eval_jaxpr/dot_general | solution.py:30
  51.5 2.2 %fusion.70 = f32[512,128]{1,0:T(8,128)S(1)} fusion(f32[512,128]{1,0:T(8,128)S(1)} %copy.26, f32[11,512,512]{2,1,0:T(8,128)} %get-tuple-element.220, s32[]{:T(128)} %get-tuple-element.211), kind=kOutput, calls=%fused_computation.2.clone.1 | convolution fusion | flops 402653184 | bytes 1573376 | tf_op jit(solution)/shard_map/while/body/eval_jaxpr/dot_general | solution.py:30
  60.5 2.2 %fusion.70 = f32[512,128]{1,0:T(8,128)S(1)} fusion(f32[512,128]{1,0:T(8,128)S(1)} %copy.26, f32[11,512,512]{2,1,0:T(8,128)} %get-tuple-element.220, s32[]{:T(128)} %get-tuple-element.211), kind=kOutput, calls=%fused_computation.2.clone.1 | convolution fusion | flops 402653184 | bytes 1573376 | tf_op jit(solution)/shard_map/while/body/eval_jaxpr/dot_general | solution.py:30
  67.9 5.2 %collective-permute-done = f32[512,128]{1,0:T(8,128)S(1)} collective-permute-done((f32[512,128]{1,0:T(8,128)S(1)}, f32[512,128]{1,0:T(8,128)S(1)}, u32[]{:S(2)}, u32[]{:S(2)}) %collective-permute-start) | collective-permute-done | bytes 262176 | tf_op jit(solution)/shard_map/ppermute | solution.py:12
  73.1 5.8 %collective-permute-done.1 = f32[512,128]{1,0:T(8,128)S(1)} collective-permute-done((f32[512,128]{1,0:T(8,128)S(1)}, f32[512,128]{1,0:T(8,128)S(1)}, u32[]{:S(2)}, u32[]{:S(2)}) %collective-permute-start.1) | collective-permute-done | bytes 262176 | tf_op jit(solution)/shard_map/ppermute | solution.py:12
  78.9 3.1 %collective-permute-start.3 = (f32[512,128]{1,0:T(8,128)S(1)}, f32[512,128]{1,0:T(8,128)S(1)}, u32[]{:S(2)}, u32[]{:S(2)}) collective-permute-start(f32[512,128]{1,0:T(8,128)S(1)} %get-tuple-element.108), channel_id=1, source_target_pairs={{0,4},{4,8},{8,12},{12,16},{16,20},{20,24},{24,28},{1,5},{5,9},{9,... | collective-permute-start | bytes 786440 | tf_op jit(solution)/shard_map/ppermute | solution.py:26
  82.2 2.5 %collective-permute-done.2 = f32[512,128]{1,0:T(8,128)S(1)} collective-permute-done((f32[512,128]{1,0:T(8,128)S(1)}, f32[512,128]{1,0:T(8,128)S(1)}, u32[]{:S(2)}, u32[]{:S(2)}) %collective-permute-start.2) | collective-permute-done | bytes 262176 | tf_op jit(solution)/shard_map/ppermute | solution.py:12
  85.3 2.7 %collective-permute-done.3 = f32[512,128]{1,0:T(8,128)S(1)} collective-permute-done((f32[512,128]{1,0:T(8,128)S(1)}, f32[512,128]{1,0:T(8,128)S(1)}, u32[]{:S(2)}, u32[]{:S(2)}) %collective-permute-start.3) | collective-permute-done | bytes 262176 | tf_op jit(solution)/shard_map/ppermute | solution.py:26
  89.2 2.5 %collective-permute-start.4 = (f32[512,128]{0,1:T(8,128)S(1)}, f32[512,128]{0,1:T(8,128)S(1)}, u32[]{:S(2)}, u32[]{:S(2)}) collective-permute-start(f32[512,128]{0,1:T(8,128)S(1)} %convolution_select_fusion.2), channel_id=1, source_target_pairs={{0,3},{1,0},{2,1},{3,2},{4,7},{5,4},{6,5},{7,6},{8,11},{9,8},{10,9... | collective-permute-start | bytes 786440 | tf_op jit(solution)/shard_map/ppermute | solution.py:12
  91.7 5.1 %collective-permute-done.4 = f32[512,128]{0,1:T(8,128)S(1)} collective-permute-done((f32[512,128]{0,1:T(8,128)S(1)}, f32[512,128]{0,1:T(8,128)S(1)}, u32[]{:S(2)}, u32[]{:S(2)}) %collective-permute-start.4) | collective-permute-done | bytes 262176 | tf_op jit(solution)/shard_map/ppermute | solution.py:12
  96.8 5.8 %collective-permute-done.5 = f32[512,128]{0,1:T(8,128)S(1)} collective-permute-done((f32[512,128]{0,1:T(8,128)S(1)}, f32[512,128]{0,1:T(8,128)S(1)}, u32[]{:S(2)}, u32[]{:S(2)}) %collective-permute-start.5) | collective-permute-done | bytes 262176 | tf_op jit(solution)/shard_map/ppermute | solution.py:12
  103.9 4.8 %collective-permute-done.6 = f32[512,128]{0,1:T(8,128)S(1)} collective-permute-done((f32[512,128]{0,1:T(8,128)S(1)}, f32[512,128]{0,1:T(8,128)S(1)}, u32[]{:S(2)}, u32[]{:S(2)}) %collective-permute-start.6) | collective-permute-done | bytes 262176 | tf_op jit(solution)/shard_map/ppermute | solution.py:12
  114.0 2.2 %collective-permute-start.12 = (f32[512]{0:T(512)S(1)}, f32[512]{0:T(512)S(1)}, u32[]{:S(2)}, u32[]{:S(2)}) collective-permute-start(f32[512]{0:T(512)S(1)} %get-tuple-element.109), channel_id=1, source_target_pairs={{0,4},{4,8},{8,12},{12,16},{16,20},{20,24},{24,28},{1,5},{5,9},{9,... | collective-permute-start | bytes 6152 | tf_op jit(solution)/shard_map/ppermute | solution.py:26
  127.4 2.8 %collective-permute-done.10 = f32[512,128]{0,1:T(8,128)S(1)} collective-permute-done((f32[512,128]{0,1:T(8,128)S(1)}, f32[512,128]{0,1:T(8,128)S(1)}, u32[]{:S(2)}, u32[]{:S(2)}) %collective-permute-start.10) | collective-permute-done | bytes 262176 | tf_op jit(solution)/shard_map/ppermute | solution.py:12
  131.7 6.2 %collective-permute-done.14 = f32[512]{0:T(512)S(1)} collective-permute-done((f32[512]{0:T(512)S(1)}, f32[512]{0:T(512)S(1)}, u32[]{:S(2)}, u32[]{:S(2)}) %collective-permute-start.14) | collective-permute-done | bytes 2080 | tf_op jit(solution)/shard_map/ppermute | solution.py:26
  139.6 7.0 %all-reduce = f32[512]{0:T(512)S(1)} all-reduce(f32[512]{0:T(512)S(1)} %bitcast.87), channel_id=2, replica_groups=mesh['tm'=8,'col'=4] {'col'}, use_global_device_ids=true, to_apply=%region_2.4.clone | all-reduce | flops 512 | bytes 4096
  148.6 3.3 %collective-permute-done.15 = f32[128]{0:T(128)S(1)} collective-permute-done((f32[128]{0:T(128)S(1)}, f32[128]{0:T(128)S(1)}, u32[]{:S(2)}, u32[]{:S(2)}) %collective-permute-start.15) | collective-permute-done | bytes 544 | tf_op jit(solution)/shard_map/ppermute | solution.py:26
  151.9 7.0 %all-gather = f32[4,1,128]{2,1,0:T(1,128)S(1)} all-gather(f32[1,1,128]{2,1,0:T(1,128)S(1)} %fusion.33), channel_id=1, replica_groups=mesh['tm'=8,'col'=4] {'col'}, dimensions={0}, use_global_device_ids=true | all-gather | bytes 2560 | tf_op jit(solution)/shard_map/all_gather | solution.py:70
  158.9 25.8 %while.27 = (s32[]{:T(128)}, f32[512]{0:T(512)S(1)}, f32[11,128]{1,0:T(8,128)S(1)}, f32[11,512,512]{2,1,0:T(8,128)}, f32[11,512]{1,0:T(8,128)S(1)}, /*index=5*/s32[]{:T(128)}, s32[]{:T(128)}, s32[]{:T(128)}) while((s32[]{:T(128)}, f32[512]{0:T(512)S(1)}, f32[11,128]{1,0:T(8,128)S(1)}, f32[11,512,512]{2,1,0:T(8,128)}, f32[11,512]{1,0:T(8,128)S(1)}, ...), condition=%wide.region_4.6_spmd, body=%wide.region_3.5_spmd.sunk | while | flops 3146242 | bytes 1065569 | solution.py:77
  (154 shorter events, 86.9 us)
Async XLA Ops:
  0.0 17.6 %copy-start = (f32[12,512]{1,0:T(8,128)S(1)}, f32[12,512]{1,0:T(8,128)}, u32[]{:S(2)}) copy-start(f32[12,512]{1,0:T(8,128)} %param.10) | copy-start | bytes 73732
  0.0 17.6 %slice-start = ((f32[12,512,512]{2,1,0:T(8,128)}), f32[1,512,512]{2,1,0:T(8,128)S(1)}, s32[]{:S(2)}) async-start(f32[12,512,512]{2,1,0:T(8,128)} %param.9), calls=%async_computation | async-start | bytes 2097152 | tf_op jit(solution)/shard_map/slice | solution.py:48
  0.0 17.7 %slice-start.1 = ((f32[12,512]{1,0:T(8,128)}), f32[1,512]{1,0:T(1,128)S(1)}, s32[]{:S(2)}) async-start(f32[12,512]{1,0:T(8,128)} %param.10), calls=%async_computation.1 | async-start | bytes 4096 | tf_op jit(solution)/shard_map/slice | solution.py:48
  67.2 5.9 %collective-permute-start = (f32[512,128]{1,0:T(8,128)S(1)}, f32[512,128]{1,0:T(8,128)S(1)}, u32[]{:S(2)}, u32[]{:S(2)}) collective-permute-start(f32[512,128]{1,0:T(8,128)S(1)} %get-tuple-element.108), channel_id=1, source_target_pairs={{0,3},{1,0},{2,1},{3,2},{4,7},{5,4},{6,5},{7,6},{8,11},{9,8},{10,9... | collective-permute-start | bytes 786440 | tf_op jit(solution)/shard_map/ppermute | solution.py:12
  73.1 5.8 %collective-permute-start.1 = (f32[512,128]{1,0:T(8,128)S(1)}, f32[512,128]{1,0:T(8,128)S(1)}, u32[]{:S(2)}, u32[]{:S(2)}) collective-permute-start(f32[512,128]{1,0:T(8,128)S(1)} %collective-permute-done), channel_id=1, source_target_pairs={{0,3},{1,0},{2,1},{3,2},{4,7},{5,4},{6,5},{7,6},{8,11},{9,8},{10,9... | collective-permute-start | bytes 786440 | tf_op jit(solution)/shard_map/ppermute | solution.py:12
  78.9 5.8 %collective-permute-start.2 = (f32[512,128]{1,0:T(8,128)S(1)}, f32[512,128]{1,0:T(8,128)S(1)}, u32[]{:S(2)}, u32[]{:S(2)}) collective-permute-start(f32[512,128]{1,0:T(8,128)S(1)} %collective-permute-done.1), channel_id=1, source_target_pairs={{0,3},{1,0},{2,1},{3,2},{4,7},{5,4},{6,5},{7,6},{8,11},{9,8},{10,9... | collective-permute-start | bytes 786440 | tf_op jit(solution)/shard_map/ppermute | solution.py:12
  78.9 9.1 %collective-permute-start.3 = (f32[512,128]{1,0:T(8,128)S(1)}, f32[512,128]{1,0:T(8,128)S(1)}, u32[]{:S(2)}, u32[]{:S(2)}) collective-permute-start(f32[512,128]{1,0:T(8,128)S(1)} %get-tuple-element.108), channel_id=1, source_target_pairs={{0,4},{4,8},{8,12},{12,16},{16,20},{20,24},{24,28},{1,5},{5,9},{9,... | collective-permute-start | bytes 786440 | tf_op jit(solution)/shard_map/ppermute | solution.py:26
  89.2 7.6 %collective-permute-start.4 = (f32[512,128]{0,1:T(8,128)S(1)}, f32[512,128]{0,1:T(8,128)S(1)}, u32[]{:S(2)}, u32[]{:S(2)}) collective-permute-start(f32[512,128]{0,1:T(8,128)S(1)} %convolution_select_fusion.2), channel_id=1, source_target_pairs={{0,3},{1,0},{2,1},{3,2},{4,7},{5,4},{6,5},{7,6},{8,11},{9,8},{10,9... | collective-permute-start | bytes 786440 | tf_op jit(solution)/shard_map/ppermute | solution.py:12
  96.8 5.8 %collective-permute-start.5 = (f32[512,128]{0,1:T(8,128)S(1)}, f32[512,128]{0,1:T(8,128)S(1)}, u32[]{:S(2)}, u32[]{:S(2)}) collective-permute-start(f32[512,128]{0,1:T(8,128)S(1)} %collective-permute-done.4), channel_id=1, source_target_pairs={{0,3},{1,0},{2,1},{3,2},{4,7},{5,4},{6,5},{7,6},{8,11},{9,8},{10,9... | collective-permute-start | bytes 786440 | tf_op jit(solution)/shard_map/ppermute | solution.py:12
  102.6 6.1 %collective-permute-start.6 = (f32[512,128]{0,1:T(8,128)S(1)}, f32[512,128]{0,1:T(8,128)S(1)}, u32[]{:S(2)}, u32[]{:S(2)}) collective-permute-start(f32[512,128]{0,1:T(8,128)S(1)} %collective-permute-done.5), channel_id=1, source_target_pairs={{0,3},{1,0},{2,1},{3,2},{4,7},{5,4},{6,5},{7,6},{8,11},{9,8},{10,9... | collective-permute-start | bytes 786440 | tf_op jit(solution)/shard_map/ppermute | solution.py:12
  102.6 9.0 %collective-permute-start.7 = (f32[512,128]{0,1:T(8,128)S(1)}, f32[512,128]{0,1:T(8,128)S(1)}, u32[]{:S(2)}, u32[]{:S(2)}) collective-permute-start(f32[512,128]{0,1:T(8,128)S(1)} %convolution_select_fusion.2), channel_id=1, source_target_pairs={{0,8},{4,12},{8,16},{12,20},{16,24},{20,28},{1,9},{5,13},{9,17},{1... | collective-permute-start | bytes 786440 | tf_op jit(solution)/shard_map/ppermute | solution.py:26
  103.9 17.6 %copy-start.2 = (u32[32]{0:T(128)S(1)}, u32[32]{0:T(128)}, u32[]{:S(2)}) copy-start(u32[32]{0:T(128)} %constant.75) | copy-start | bytes 388
  112.3 5.9 %collective-permute-start.8 = (f32[512,128]{0,1:T(8,128)S(1)}, f32[512,128]{0,1:T(8,128)S(1)}, u32[]{:S(2)}, u32[]{:S(2)}) collective-permute-start(f32[512,128]{0,1:T(8,128)S(1)} %convolution_select_fusion.1), channel_id=1, source_target_pairs={{0,3},{1,0},{2,1},{3,2},{4,7},{5,4},{6,5},{7,6},{8,11},{9,8},{10,9... | collective-permute-start | bytes 786440 | tf_op jit(solution)/shard_map/ppermute | solution.py:12
  114.0 5.2 %collective-permute-start.12 = (f32[512]{0:T(512)S(1)}, f32[512]{0:T(512)S(1)}, u32[]{:S(2)}, u32[]{:S(2)}) collective-permute-start(f32[512]{0:T(512)S(1)} %get-tuple-element.109), channel_id=1, source_target_pairs={{0,4},{4,8},{8,12},{12,16},{16,20},{20,24},{24,28},{1,5},{5,9},{9,... | collective-permute-start | bytes 6152 | tf_op jit(solution)/shard_map/ppermute | solution.py:26
  118.2 5.8 %collective-permute-start.9 = (f32[512,128]{0,1:T(8,128)S(1)}, f32[512,128]{0,1:T(8,128)S(1)}, u32[]{:S(2)}, u32[]{:S(2)}) collective-permute-start(f32[512,128]{0,1:T(8,128)S(1)} %collective-permute-done.8), channel_id=1, source_target_pairs={{0,3},{1,0},{2,1},{3,2},{4,7},{5,4},{6,5},{7,6},{8,11},{9,8},{10,9... | collective-permute-start | bytes 786440 | tf_op jit(solution)/shard_map/ppermute | solution.py:12
  120.2 5.1 %collective-permute-start.13 = (f32[512]{0:T(512)S(1)}, f32[512]{0:T(512)S(1)}, u32[]{:S(2)}, u32[]{:S(2)}) collective-permute-start(f32[512]{0:T(512)S(1)} %add_select_fusion.2), channel_id=1, source_target_pairs={{0,8},{4,12},{8,16},{12,20},{16,24},{20,28},{1,9},{5,13},{9,17},{1... | collective-permute-start | bytes 6152 | tf_op jit(solution)/shard_map/ppermute | solution.py:26
  122.7 15.8 %collective-permute-start.11 = (f32[512,128]{0,1:T(8,128)S(1)}, f32[512,128]{0,1:T(8,128)S(1)}, u32[]{:S(2)}, u32[]{:S(2)}) collective-permute-start(f32[512,128]{0,1:T(8,128)S(1)} %convolution_select_fusion.1), channel_id=1, source_target_pairs={{0,16},{4,20},{8,24},{12,28},{1,17},{5,21},{9,25},{13,29},{2,18},{... | collective-permute-start | bytes 786440 | tf_op jit(solution)/shard_map/ppermute | solution.py:26
  124.0 6.1 %collective-permute-start.10 = (f32[512,128]{0,1:T(8,128)S(1)}, f32[512,128]{0,1:T(8,128)S(1)}, u32[]{:S(2)}, u32[]{:S(2)}) collective-permute-start(f32[512,128]{0,1:T(8,128)S(1)} %collective-permute-done.9), channel_id=1, source_target_pairs={{0,3},{1,0},{2,1},{3,2},{4,7},{5,4},{6,5},{7,6},{8,11},{9,8},{10,9... | collective-permute-start | bytes 786440 | tf_op jit(solution)/shard_map/ppermute | solution.py:12
  125.9 13.4 %copy-start.1 = (f32[128]{0:T(128)S(1)}, f32[128]{0:T(128)}, u32[]{:S(2)}) copy-start(f32[128]{0:T(128)} %param.11) | copy-start | bytes 1540
  125.9 12.0 %collective-permute-start.14 = (f32[512]{0:T(512)S(1)}, f32[512]{0:T(512)S(1)}, u32[]{:S(2)}, u32[]{:S(2)}) collective-permute-start(f32[512]{0:T(512)S(1)} %add_select_fusion.1), channel_id=1, source_target_pairs={{0,16},{4,20},{8,24},{12,28},{1,17},{5,21},{9,25},{13,29},{2,18},{... | collective-permute-start | bytes 6152 | tf_op jit(solution)/shard_map/ppermute | solution.py:26
  146.7 5.2 %collective-permute-start.15 = (f32[128]{0:T(128)S(1)}, f32[128]{0:T(128)S(1)}, u32[]{:S(2)}, u32[]{:S(2)}) collective-permute-start(f32[128]{0:T(128)S(1)} %dynamic-slice_add_fusion), channel_id=1, source_target_pairs={{0,4},{4,8},{8,12},{12,16},{16,20},{20,24},{24,28},{1,5},{5,9},{9,... | collective-permute-start | bytes 1544 | tf_op jit(solution)/shard_map/ppermute | solution.py:26
